TPU v7x, 128 devices: a whole 4x4x4 slice. The times are simulated.
128 devices in a mesh: gx: 16 (over y, x_hi, core), gy: 8 (over z, x_lo).
Axes of the slice: x: 4 (x_hi: 2, x_lo: 2; x = x_hi * 2 + x_lo), y: 4, z: 4, core: 2. Of those that a mesh axis runs over, the one named last changes fastest.
Arguments:
- forces: float32 [3, 24, 32, 64, 128], P(None, None, 'gx', 'gy'), may hold values from -6 to 6
- levels: int32 [32, 64, 128], P('gx', 'gy'), may hold values from 0 to 15
- supports: int32 [32, 64, 128], P('gx', 'gy'), may hold values 0 or 1
Outputs:
- filtered: float32 [32, 64, 128], P('gx', 'gy')
All inputs are finite; a program needn't handle non-finite values. No bound on the sum of `supports` on one device may be relied on, other than what follows from the above.
Results may differ from a plain program's by a relative error of at most 0.0001.
Values sent between devices are 32-bit elements; how exact they have to be, the bound alone decides.
A program may use at most 128 MiB of HBM per device.

v0:
```python
import math
import jax
import jax.numpy as jnp
import numpy as np
from jax import lax
from jax.sharding import PartitionSpec as P

CASES = 24
LEVELS = 16
ITERS = 2
load_factor = 0.2


def from_behind(value, axis, steps):
    count = lax.axis_size(axis)
    leading, last = (max(0, -steps), min(count, count - steps))
    return lax.ppermute(value, axis, [(source, source + steps) for source in range(leading, last)])


def extended_2(x, sides, width):
    for axis, dim in sides:
        count, length = (lax.axis_size(axis), x.shape[dim])
        up = [(i, (i + 1) % count) for i in range(count - 1)]
        down = [(j, i) for i, j in up]
        last = lax.slice_in_dim(x, length - width, length, axis=dim)
        leading = lax.slice_in_dim(x, 0, width, axis=dim)
        before = lax.ppermute(last, axis, up)
        after = lax.ppermute(leading, axis, down)
        x = jnp.concatenate([before, x, after], axis=dim)
    return x


def element_matrix():
    poisson = 0.3
    lame_first = poisson / ((1.0 + poisson) * (1.0 - 2.0 * poisson))
    lame_shear = 1.0 / (2.0 * (1.0 + poisson))
    elastic = np.zeros((6, 6))
    elastic[:3, :3] = lame_first
    for position in range(3):
        elastic[position, position] += 2.0 * lame_shear
        elastic[position + 3, position + 3] = lame_shear
    points = [0.5 - 0.5 / math.sqrt(3.0), 0.5 + 0.5 / math.sqrt(3.0)]
    matrix = np.zeros((24, 24))
    for point_x in points:
        for point_y in points:
            for point_z in points:
                coords = (point_x, point_y, point_z)
                strain = np.zeros((6, 24))
                for corner in range(8):
                    corner_bits = (corner >> 2 & 1, corner >> 1 & 1, corner & 1)
                    shape_values = [
                        coords[axis_n] if corner_bits[axis_n] else 1.0 - coords[axis_n]
                        for axis_n in range(3)
                    ]
                    slopes = [1.0 if corner_bits[axis_n] else -1.0 for axis_n in range(3)]
                    slope_x = slopes[0] * shape_values[1] * shape_values[2]
                    slope_y = shape_values[0] * slopes[1] * shape_values[2]
                    slope_z = shape_values[0] * shape_values[1] * slopes[2]
                    offset = 3 * corner
                    strain[0, offset] = slope_x
                    strain[1, offset + 1] = slope_y
                    strain[2, offset + 2] = slope_z
                    strain[3, offset] = slope_y
                    strain[3, offset + 1] = slope_x
                    strain[4, offset + 1] = slope_z
                    strain[4, offset + 2] = slope_y
                    strain[5, offset] = slope_z
                    strain[5, offset + 2] = slope_x
                matrix = matrix + strain.T @ elastic @ strain / 8.0
    return matrix


def corner_stack(field_in, lead_in, span_x, span_y, span_z):
    pieces = []
    for corner in range(8):
        step_x, step_y, step_z = (corner >> 2 & 1, corner >> 1 & 1, corner & 1)
        pieces.append(
            field_in[
                :,
                :,
                lead_in + step_x : lead_in + step_x + span_x,
                lead_in + step_y : lead_in + step_y + span_y,
                lead_in + step_z : lead_in + step_z + span_z,
            ]
        )
    stacked = jnp.stack(pieces, 0)
    return stacked.reshape((24,) + stacked.shape[2:])


def element_forces(extended, stiff_ext, element_stiff):
    span_x, span_y, span_z = (extended.shape[2] - 2, extended.shape[3] - 2, extended.shape[4] - 2)
    outputs = []
    for first_case in range(0, extended.shape[1], 6):
        case_group = extended[:, first_case : first_case + 6]
        gathered = corner_stack(case_group, 0, span_x + 1, span_y + 1, span_z + 1)
        product = (
            jnp.einsum("ab,bcxyz->acxyz", element_stiff, gathered, precision=lax.Precision.HIGHEST)
            * stiff_ext
        )
        product = product.reshape((8, 3) + product.shape[1:])
        summed = jnp.zeros((3, case_group.shape[1], span_x, span_y, span_z), jnp.float32)
        for corner in range(8):
            step_x, step_y, step_z = (corner >> 2 & 1, corner >> 1 & 1, corner & 1)
            summed = (
                summed
                + product[corner][
                    :,
                    :,
                    1 - step_x : 1 - step_x + span_x,
                    1 - step_y : 1 - step_y + span_y,
                    1 - step_z : 1 - step_z + span_z,
                ]
            )
        outputs.append(summed)
    return jnp.concatenate(outputs, 1)


def element_energy(extended, element_stiff):
    span_x, span_y, span_z = (extended.shape[2] - 2, extended.shape[3] - 2, extended.shape[4] - 2)
    summed = jnp.zeros((span_x, span_y, span_z), jnp.float32)
    for first_case in range(0, extended.shape[1], 6):
        case_group = extended[:, first_case : first_case + 6]
        gathered = corner_stack(case_group, 1, span_x, span_y, span_z)
        product = jnp.einsum(
            "ab,bcxyz->acxyz", element_stiff, gathered, precision=lax.Precision.HIGHEST
        )
        summed = summed + jnp.sum(gathered * product, axis=(0, 1))
    return summed


def node_diagonal(stiff_ext, free_mask, element_stiff):
    span_x, span_y, span_z = free_mask.shape
    parts = []
    for component in range(3):
        summed = jnp.zeros((span_x, span_y, span_z), jnp.float32)
        for corner in range(8):
            step_x, step_y, step_z = (corner >> 2 & 1, corner >> 1 & 1, corner & 1)
            summed = (
                summed
                + stiff_ext[
                    1 - step_x : 1 - step_x + span_x,
                    1 - step_y : 1 - step_y + span_y,
                    1 - step_z : 1 - step_z + span_z,
                ]
                * element_stiff[3 * corner + component, 3 * corner + component]
            )
        parts.append(summed)
    diagonal = jnp.stack(parts, 0)[:, None]
    return 1.0 / (free_mask * diagonal + (1.0 - free_mask))


def block_gram(first_field, second_field):
    return jnp.einsum("kcxyz,kdxyz->cd", first_field, second_field, precision=lax.Precision.HIGHEST)


def combine(field_in, mixing):
    return jnp.einsum("kcxyz,cd->kdxyz", field_in, mixing, precision=lax.Precision.HIGHEST)


def cone_filter(rimmed, density):
    span_x, span_y, span_z = density.shape
    numerator = jnp.zeros((span_x, span_y, span_z), jnp.float32)
    denominator = jnp.zeros((span_x, span_y, span_z), jnp.float32)
    for shift_x in range(-2, 3):
        for shift_y in range(-2, 3):
            for shift_z in range(-2, 3):
                weight = 2.5 - math.sqrt(shift_x * shift_x + shift_y * shift_y + shift_z * shift_z)
                if weight > 0.0:
                    window = rimmed[
                        :,
                        2 + shift_x : 2 + shift_x + span_x,
                        2 + shift_y : 2 + shift_y + span_y,
                        2 + shift_z : 2 + shift_z + span_z,
                    ]
                    numerator = numerator + weight * window[0]
                    denominator = denominator + weight * window[1]
    return numerator / (density * denominator)


def local(forces, levels, supports):
    element_stiff = jnp.asarray(element_matrix(), jnp.float32)
    free_mask = (1 - supports).astype(jnp.float32)
    density = 0.3 + 0.7 * levels.astype(jnp.float32) / (LEVELS - 1)
    stiffness = density**3
    below_x = from_behind(stiffness[-1:], "gx", 1)
    widened = jnp.concatenate([below_x, stiffness], 0)
    below_y = from_behind(widened[:, -1:], "gy", 1)
    widened = jnp.concatenate([below_y, widened], 1)
    stiff_ext = jnp.pad(widened, ((0, 0), (0, 0), (1, 0)))
    inverse = node_diagonal(stiff_ext, free_mask, element_stiff)
    load_field = load_factor * free_mask * forces
    solution = jnp.zeros_like(load_field)
    residual = load_field
    direction = inverse * residual
    kept_rims = []
    alphas_kept = []
    for iteration in range(ITERS):
        extended = extended_2(free_mask * direction, (("gx", 2), ("gy", 3)), 1)
        extended = jnp.pad(extended, ((0, 0), (0, 0), (0, 0), (0, 0), (1, 1)))
        applied = (
            free_mask * element_forces(extended, stiff_ext, element_stiff)
            + (1.0 - free_mask) * direction
        )
        image_field, extended = (applied, extended)
        kept_rims.append(extended)
        curvature, along_dir = lax.psum(
            (block_gram(direction, image_field), block_gram(direction, residual)), ("gx", "gy")
        )
        factor = jnp.linalg.cholesky(curvature)
        step_alpha = jax.scipy.linalg.cho_solve((factor, True), along_dir)
        alphas_kept.append(step_alpha)
        solution = solution + combine(direction, step_alpha)
        residual = residual - combine(image_field, step_alpha)
        if iteration + 1 < ITERS:
            scaled_res = inverse * residual
            coupling = lax.psum(block_gram(image_field, scaled_res), ("gx", "gy"))
            step_beta = -jax.scipy.linalg.cho_solve((factor, True), coupling)
            direction = scaled_res + combine(direction, step_beta)
    masked_sol = free_mask * solution
    above_x = from_behind(masked_sol[:, :, :1], "gx", -1)
    sol_wide = jnp.concatenate([masked_sol, above_x], 2)
    above_y = from_behind(sol_wide[:, :, :, :1], "gy", -1)
    sol_wide = jnp.concatenate([sol_wide, above_y], 3)
    sol_ext = jnp.pad(sol_wide, ((0, 0), (0, 0), (1, 0), (1, 0), (1, 1)))
    energy = element_energy(sol_ext, element_stiff)
    sensitivity = -3.0 * density**2 * energy / CASES
    stacked = jnp.stack([density * sensitivity, jnp.ones_like(density)], 0)
    rimmed = extended_2(stacked, (("gx", 1), ("gy", 2)), 2)
    rimmed = jnp.pad(rimmed, ((0, 0), (0, 0), (0, 0), (2, 2)))
    return cone_filter(rimmed, density)


def solution(mesh):
    return jax.shard_map(
        local,
        mesh=mesh,
        in_specs=(P(None, None, "gx", "gy", None), P("gx", "gy", None), P("gx", "gy", None)),
        out_specs=P("gx", "gy", None),
        check_vma=False,
    )
```

profile of v0, /device:TPU:8, one launch (start us, length us, event | category | flops | bytes accessed | tf_op | source)
XLA Modules:
  0.0 547.2 jit_solution(6883320357306443744)
XLA Ops:
  2.6 5.4 collective-permute-done
  17.1 6.0 %collective-permute-start.3 = (f32[3,24,1,8,128]{4,0,3,2,1:T(4,128)S(1)}, f32[3,24,1,8,128]{4,0,3,2,1:T(4,128)S(1)}, u32[]{:S(2)}, u32[]{:S(2)}) collective-permute-start(f32[3,24,1,8,128]{4,0,3,2,1:T(4,128)S(1)} %get-tuple-element.102), channel_id=1, source_target_pairs={{8,0},{16,8},{24,16},{32,24},{40,32},{48,40},{56,48},{64,56},{72,6... | collective-permute-start | bytes 884744 | tf_op jit(solution)/shard_map/ppermute | solution.py:28
  36.6 7.4 %collective-permute-done.5 = f32[3,24,4,1,128]{4,0,3,2,1:T(4,128)S(1)} collective-permute-done((f32[3,24,4,1,128]{4,0,3,2,1:T(4,128)S(1)}, f32[3,24,4,1,128]{4,0,3,2,1:T(4,128)S(1)}, u32[]{:S(2)}, u32[]{:S(2)}) %collective-permute-start.5) | collective-permute-done | bytes 147488 | tf_op jit(solution)/shard_map/ppermute | solution.py:28
  67.9 7.6 %reshape.547 = f32[24,6,3,9,129]{4,0,3,2,1:T(8,128)} reshape(f32[8,3,6,3,9,129]{5,1,0,4,3,2:T(4,128)} %copy.32) | data formatting | bytes 4012416 | tf_op jit(solution)/shard_map/reshape | solution.py:87
  77.8 6.4 %copy.35 = f32[8,3,6,3,9,129]{5,1,0,4,3,2:T(4,128)} copy(f32[8,3,6,3,9,129]{5,1,4,3,2,0:T(4,128)} %fusion.46) | data formatting | bytes 4012416 | tf_op jit(solution)/shard_map/stack | solution.py:86
  84.2 7.4 %reshape.550 = f32[24,6,3,9,129]{4,0,3,2,1:T(8,128)} reshape(f32[8,3,6,3,9,129]{5,1,0,4,3,2:T(4,128)} %copy.35) | data formatting | bytes 4012416 | tf_op jit(solution)/shard_map/reshape | solution.py:87
  91.7 7.8 %multiply_bitcast_fusion.7 = f32[24,6,3,9,129]{4,0,3,2,1:T(8,128)} fusion(f32[24,6,3,9,129]{4,0,3,2,1:T(8,128)} %reshape.547, f32[24,24,1,1,1]{1,0,4,3,2:T(8,128)S(1)} %copy-done.11, f32[3,9,129]{2,1,0:T(8,128)S(1)} %pad.20), kind=kOutput, calls=%fused_computation.25 | convolution fusion | flops 144948528 | bytes 4028652 | tf_op jit(solution)/shard_map/ab,bcxyz->acxyz/dot_general | solution.py:97
  99.4 5.0 multiply_bitcast_fusion.4
  108.4 7.7 %reshape.549 = f32[24,6,3,9,129]{4,0,3,2,1:T(8,128)} reshape(f32[8,3,6,3,9,129]{5,1,0,4,3,2:T(4,128)} %copy.34) | data formatting | bytes 4012416 | tf_op jit(solution)/shard_map/reshape | solution.py:87
  116.1 7.6 %multiply_bitcast_fusion.5 = f32[24,6,3,9,129]{4,0,3,2,1:T(8,128)} fusion(f32[24,6,3,9,129]{4,0,3,2,1:T(8,128)} %reshape.549, f32[24,24,1,1,1]{1,0,4,3,2:T(8,128)S(1)} %copy-done.11, f32[3,9,129]{2,1,0:T(8,128)S(1)} %pad.20), kind=kOutput, calls=%fused_computation.23 | convolution fusion | flops 144948528 | bytes 4028652 | tf_op jit(solution)/shard_map/ab,bcxyz->acxyz/dot_general | solution.py:97
  123.7 6.5 %copy.33 = f32[8,3,6,3,9,129]{5,1,0,4,3,2:T(4,128)} copy(f32[8,3,6,3,9,129]{5,1,4,3,2,0:T(4,128)} %copy-done.6) | data formatting | bytes 4012416 | tf_op jit(solution)/shard_map/stack | solution.py:86
  130.2 7.4 %reshape.548 = f32[24,6,3,9,129]{4,0,3,2,1:T(8,128)} reshape(f32[8,3,6,3,9,129]{5,1,0,4,3,2:T(4,128)} %copy.33) | data formatting | bytes 4012416 | tf_op jit(solution)/shard_map/reshape | solution.py:87
  137.6 5.3 multiply_bitcast_fusion.6
  142.9 5.7 %slice_add_fusion.28 = (f32[3,6,2,8,128]{4,0,3,2,1:T(4,128)S(1)}, f32[3,6,2,8,128]{4,0,3,2,1:T(4,128)S(1)}) fusion(f32[24,6,3,9,129]{4,0,3,2,1:T(8,128)} %multiply_bitcast_fusion.4, f32[24,6,3,9,129]{4,0,3,2,1:T(8,128)} %multiply_bitcast_fusion.5), kind=kLoop, calls=%fused_computation.312 | loop fusion | flops 516096 | bytes 2654208 | tf_op jit(solution)/shard_map/add | solution.py:105
  156.1 67.5 %all-reduce.7 = (f32[24,24]{1,0:T(8,128)S(1)}, f32[24,24]{0,1:T(8,128)S(1)}) all-reduce(f32[24,24]{1,0:T(8,128)S(1)} %convolution_bitcast_fusion.5, f32[24,24]{0,1:T(8,128)S(1)} %convolution_bitcast_fusion.6), channel_id=1, replica_groups=mesh['gx'=16,'gy'=8] {'gx','gy'}, use_global_device_ids=true, to_apply=%region_3.5 | all-reduce | flops 1152 | bytes 9216 | tf_op jit(solution)/shard_map/psum | solution.py:206
  233.4 62.4 %psum.37 = f32[24,24]{1,0:T(8,128)S(1)} all-reduce(f32[24,24]{1,0:T(8,128)S(1)} %convolution_bitcast_fusion.3), channel_id=1, replica_groups=mesh['gx'=16,'gy'=8] {'gx','gy'}, use_global_device_ids=true, to_apply=%region_4.7 | all-reduce | flops 576 | bytes 4608 | tf_op jit(solution)/shard_map/psum | solution.py:216
  300.2 6.0 %collective-permute-start.7 = (f32[3,24,1,8,128]{4,0,3,2,1:T(4,128)S(1)}, f32[3,24,1,8,128]{4,0,3,2,1:T(4,128)S(1)}, u32[]{:S(2)}, u32[]{:S(2)}) collective-permute-start(f32[3,24,1,8,128]{4,0,3,2,1:T(4,128)S(1)} %get-tuple-element.100), channel_id=1, source_target_pairs={{8,0},{16,8},{24,16},{32,24},{40,32},{48,40},{56,48},{64,56},{72,6... | collective-permute-start | bytes 884744 | tf_op jit(solution)/shard_map/ppermute | solution.py:28
  319.2 7.2 %collective-permute-done.9 = f32[3,24,4,1,128]{4,0,3,2,1:T(4,128)S(1)} collective-permute-done((f32[3,24,4,1,128]{4,0,3,2,1:T(4,128)S(1)}, f32[3,24,4,1,128]{4,0,3,2,1:T(4,128)S(1)}, u32[]{:S(2)}, u32[]{:S(2)}) %collective-permute-start.9) | collective-permute-done | bytes 147488 | tf_op jit(solution)/shard_map/ppermute | solution.py:28
  350.3 7.4 %reshape.551 = f32[24,6,3,9,129]{4,0,3,2,1:T(8,128)} reshape(f32[8,3,6,3,9,129]{5,1,0,4,3,2:T(4,128)} %copy.47) | data formatting | bytes 4012416 | tf_op jit(solution)/shard_map/reshape | solution.py:87
  357.7 5.4 multiply_bitcast_fusion.3
  366.0 6.4 %copy.50 = f32[8,3,6,3,9,129]{5,1,0,4,3,2:T(4,128)} copy(f32[8,3,6,3,9,129]{5,1,4,3,2,0:T(4,128)} %fusion.14) | data formatting | bytes 4012416 | tf_op jit(solution)/shard_map/stack | solution.py:86
  372.4 7.4 %reshape.554 = f32[24,6,3,9,129]{4,0,3,2,1:T(8,128)} reshape(f32[8,3,6,3,9,129]{5,1,0,4,3,2:T(4,128)} %copy.50) | data formatting | bytes 4012416 | tf_op jit(solution)/shard_map/reshape | solution.py:87
  379.8 5.3 multiply_bitcast_fusion
  385.6 6.4 %copy.49 = f32[8,3,6,3,9,129]{5,1,0,4,3,2:T(4,128)} copy(f32[8,3,6,3,9,129]{5,1,4,3,2,0:T(4,128)} %copy-done.7) | data formatting | bytes 4012416 | tf_op jit(solution)/shard_map/stack | solution.py:86
  392.0 7.4 %reshape.553 = f32[24,6,3,9,129]{4,0,3,2,1:T(8,128)} reshape(f32[8,3,6,3,9,129]{5,1,0,4,3,2:T(4,128)} %copy.49) | data formatting | bytes 4012416 | tf_op jit(solution)/shard_map/reshape | solution.py:87
  399.3 5.3 multiply_bitcast_fusion.1
  405.1 6.5 %copy.48 = f32[8,3,6,3,9,129]{5,1,0,4,3,2:T(4,128)} copy(f32[8,3,6,3,9,129]{5,1,4,3,2,0:T(4,128)} %copy-done.8) | data formatting | bytes 4012416 | tf_op jit(solution)/shard_map/stack | solution.py:86
  411.6 7.6 %reshape.552 = f32[24,6,3,9,129]{4,0,3,2,1:T(8,128)} reshape(f32[8,3,6,3,9,129]{5,1,0,4,3,2:T(4,128)} %copy.48) | data formatting | bytes 4012416 | tf_op jit(solution)/shard_map/reshape | solution.py:87
  419.2 5.3 multiply_bitcast_fusion.2
  426.6 64.6 %all-reduce.6 = (f32[24,24]{1,0:T(8,128)S(1)}, f32[24,24]{0,1:T(8,128)S(1)}) all-reduce(f32[24,24]{1,0:T(8,128)S(1)} %convolution_bitcast_fusion.1, f32[24,24]{0,1:T(8,128)S(1)} %convolution_bitcast_fusion.2), channel_id=1, replica_groups=mesh['gx'=16,'gy'=8] {'gx','gy'}, use_global_device_ids=true, to_apply=%region_6.9 | all-reduce | flops 1152 | bytes 9216 | tf_op jit(solution)/shard_map/psum | solution.py:206
  507.3 5.9 %collective-permute-done.11 = f32[3,24,3,1,128]{4,1,3,2,0:T(8,128)S(1)} collective-permute-done((f32[3,24,3,1,128]{4,1,3,2,0:T(8,128)S(1)}, f32[3,24,3,1,128]{4,1,3,2,0:T(8,128)S(1)}, u32[]{:S(2)}, u32[]{:S(2)}) %collective-permute-start.11) | collective-permute-done | bytes 110624 | tf_op jit(solution)/shard_map/ppermute | solution.py:17
  530.6 5.5 %collective-permute-done.12 = f32[2,2,8,128]{3,2,1,0:T(8,128)S(1)} collective-permute-done((f32[2,2,8,128]{3,2,1,0:T(8,128)S(1)}, f32[2,2,8,128]{3,2,1,0:T(8,128)S(1)}, u32[]{:S(2)}, u32[]{:S(2)}) %collective-permute-start.12) | collective-permute-done | bytes 16416 | tf_op jit(solution)/shard_map/ppermute | solution.py:27
  (160 shorter events, 163.2 us)
Async XLA Ops:
  0.7 7.3 %collective-permute-start = (f32[1,8,128]{2,1,0:T(8,128)S(1)}, f32[1,8,128]{2,1,0:T(8,128)S(1)}, u32[]{:S(2)}, u32[]{:S(2)}) collective-permute-start(f32[1,8,128]{2,1,0:T(8,128)S(1)} %slice.2141), channel_id=1, source_target_pairs={{0,8},{8,16},{16,24},{24,32},{32,40},{40,48},{48,56},{56,64},{64,7... | collective-permute-start | bytes 12296 | tf_op jit(solution)/shard_map/ppermute | solution.py:17
  8.0 4.7 collective-permute-start.1
  15.1 12.7 %collective-permute-start.2 = (f32[3,24,1,8,128]{4,0,3,2,1:T(4,128)S(1)}, f32[3,24,1,8,128]{4,0,3,2,1:T(4,128)S(1)}, u32[]{:S(2)}, u32[]{:S(2)}) collective-permute-start(f32[3,24,1,8,128]{4,0,3,2,1:T(4,128)S(1)} %get-tuple-element.101), channel_id=1, source_target_pairs={{0,8},{8,16},{16,24},{24,32},{32,40},{40,48},{48,56},{56,64},{64,7... | collective-permute-start | bytes 884744 | tf_op jit(solution)/shard_map/ppermute | solution.py:27
  17.1 11.3 %collective-permute-start.3 = (f32[3,24,1,8,128]{4,0,3,2,1:T(4,128)S(1)}, f32[3,24,1,8,128]{4,0,3,2,1:T(4,128)S(1)}, u32[]{:S(2)}, u32[]{:S(2)}) collective-permute-start(f32[3,24,1,8,128]{4,0,3,2,1:T(4,128)S(1)} %get-tuple-element.102), channel_id=1, source_target_pairs={{8,0},{16,8},{24,16},{32,24},{40,32},{48,40},{56,48},{64,56},{72,6... | collective-permute-start | bytes 884744 | tf_op jit(solution)/shard_map/ppermute | solution.py:28
  28.5 8.1 %collective-permute-start.4 = (f32[3,24,4,1,128]{4,0,3,2,1:T(4,128)S(1)}, f32[3,24,4,1,128]{4,0,3,2,1:T(4,128)S(1)}, u32[]{:S(2)}, u32[]{:S(2)}) collective-permute-start(f32[3,24,4,1,128]{4,0,3,2,1:T(4,128)S(1)} %get-tuple-element.79), channel_id=1, source_target_pairs={{0,1},{1,2},{2,3},{3,4},{4,5},{5,6},{6,7},{8,9},{9,10},{10,11},{11... | collective-permute-start | bytes 442376 | tf_op jit(solution)/shard_map/ppermute | solution.py:27
  32.7 11.3 %collective-permute-start.5 = (f32[3,24,4,1,128]{4,0,3,2,1:T(4,128)S(1)}, f32[3,24,4,1,128]{4,0,3,2,1:T(4,128)S(1)}, u32[]{:S(2)}, u32[]{:S(2)}) collective-permute-start(f32[3,24,4,1,128]{4,0,3,2,1:T(4,128)S(1)} %get-tuple-element.80), channel_id=1, source_target_pairs={{1,0},{2,1},{3,2},{4,3},{5,4},{6,5},{7,6},{9,8},{10,9},{11,10},{12... | collective-permute-start | bytes 442376 | tf_op jit(solution)/shard_map/ppermute | solution.py:28
  48.2 7.3 %copy-start.1 = (f32[3,24,4,10,130]{4,0,3,2,1:T(4,128)}, f32[3,24,4,10,130]{4,0,3,2,1:T(4,128)S(1)}, u32[]{:S(2)}) copy-start(f32[3,24,4,10,130]{4,0,3,2,1:T(4,128)S(1)} %select_maximum_fusion.4) | copy-start | bytes 4492804
  56.9 2.3 copy-start.3
  59.2 2.4 copy-start.5
  61.6 2.3 copy-start.6
  84.2 7.4 %copy-start.11 = (f32[24,24,1,1,1]{1,0,4,3,2:T(8,128)S(1)}, f32[24,24,1,1,1]{1,0,4,3,2:T(8,128)}, u32[]{:S(2)}) copy-start(f32[24,24,1,1,1]{1,0,4,3,2:T(8,128)} %constant.139) | copy-start | bytes 6916
  91.6 7.8 %copy-start.2 = (f32[24,6,3,9,129]{4,0,3,2,1:T(8,128)S(1)}, f32[24,6,3,9,129]{4,0,3,2,1:T(8,128)}, u32[]{:S(2)}) copy-start(f32[24,6,3,9,129]{4,0,3,2,1:T(8,128)} %reshape.550) | copy-start | bytes 6018628
  91.6 12.8 %slice-start = ((s8[5308416]{0:T(1024)(128)(4,1)}), s8[4194304]{0:T(1024)(128)(4,1)S(1)}, s32[]{:S(2)}) async-start(s8[5308416]{0:T(1024)(128)(4,1)} %bitcast.1302), calls=%async_computation | async-start | bytes 8388608
  99.4 5.0 slice-start.1
  142.9 9.7 %copy-start.9 = (f32[3,24,2,8,128]{4,3,2,1,0:T(8,128)S(1)}, f32[3,24,2,8,128]{4,3,2,1,0:T(8,128)}, u32[]{:S(2)}) copy-start(f32[3,24,2,8,128]{4,3,2,1,0:T(8,128)} %param.7) | copy-start | bytes 1769476
  297.1 19.0 %copy-start.10 = (f32[3,24,2,8,128]{4,0,3,2,1:T(4,128)S(1)}, f32[3,24,2,8,128]{4,0,3,2,1:T(4,128)}, u32[]{:S(2)}) copy-start(f32[3,24,2,8,128]{4,0,3,2,1:T(4,128)} %get-tuple-element.14) | copy-start | bytes 1769476
  297.9 11.9 %collective-permute-start.6 = (f32[3,24,1,8,128]{4,0,3,2,1:T(4,128)S(1)}, f32[3,24,1,8,128]{4,0,3,2,1:T(4,128)S(1)}, u32[]{:S(2)}, u32[]{:S(2)}) collective-permute-start(f32[3,24,1,8,128]{4,0,3,2,1:T(4,128)S(1)} %get-tuple-element.99), channel_id=1, source_target_pairs={{0,8},{8,16},{16,24},{24,32},{32,40},{40,48},{48,56},{56,64},{64,7... | collective-permute-start | bytes 884744 | tf_op jit(solution)/shard_map/ppermute | solution.py:27
  300.2 11.3 %collective-permute-start.7 = (f32[3,24,1,8,128]{4,0,3,2,1:T(4,128)S(1)}, f32[3,24,1,8,128]{4,0,3,2,1:T(4,128)S(1)}, u32[]{:S(2)}, u32[]{:S(2)}) collective-permute-start(f32[3,24,1,8,128]{4,0,3,2,1:T(4,128)S(1)} %get-tuple-element.100), channel_id=1, source_target_pairs={{8,0},{16,8},{24,16},{32,24},{40,32},{48,40},{56,48},{64,56},{72,6... | collective-permute-start | bytes 884744 | tf_op jit(solution)/shard_map/ppermute | solution.py:28
  311.7 7.5 %collective-permute-start.8 = (f32[3,24,4,1,128]{4,0,3,2,1:T(4,128)S(1)}, f32[3,24,4,1,128]{4,0,3,2,1:T(4,128)S(1)}, u32[]{:S(2)}, u32[]{:S(2)}) collective-permute-start(f32[3,24,4,1,128]{4,0,3,2,1:T(4,128)S(1)} %get-tuple-element.77), channel_id=1, source_target_pairs={{0,1},{1,2},{2,3},{3,4},{4,5},{5,6},{6,7},{8,9},{9,10},{10,11},{11... | collective-permute-start | bytes 442376 | tf_op jit(solution)/shard_map/ppermute | solution.py:27
  314.8 11.6 %collective-permute-start.9 = (f32[3,24,4,1,128]{4,0,3,2,1:T(4,128)S(1)}, f32[3,24,4,1,128]{4,0,3,2,1:T(4,128)S(1)}, u32[]{:S(2)}, u32[]{:S(2)}) collective-permute-start(f32[3,24,4,1,128]{4,0,3,2,1:T(4,128)S(1)} %get-tuple-element.78), channel_id=1, source_target_pairs={{1,0},{2,1},{3,2},{4,3},{5,4},{6,5},{7,6},{9,8},{10,9},{11,10},{12... | collective-permute-start | bytes 442376 | tf_op jit(solution)/shard_map/ppermute | solution.py:28
  330.6 7.3 %copy-start = (f32[3,24,4,10,130]{4,0,3,2,1:T(4,128)}, f32[3,24,4,10,130]{4,0,3,2,1:T(4,128)S(1)}, u32[]{:S(2)}) copy-start(f32[3,24,4,10,130]{4,0,3,2,1:T(4,128)S(1)} %select_maximum_fusion) | copy-start | bytes 4492804
  339.3 2.3 copy-start.4
  341.6 2.4 copy-start.7
  344.0 2.3 copy-start.8
  498.1 7.6 %collective-permute-start.10 = (f32[3,24,1,8,128]{4,1,3,2,0:T(8,128)S(1)}, f32[3,24,1,8,128]{4,1,3,2,0:T(8,128)S(1)}, u32[]{:S(2)}, u32[]{:S(2)}) collective-permute-start(f32[3,24,1,8,128]{4,1,3,2,0:T(8,128)S(1)} %slice.2277), channel_id=1, source_target_pairs={{8,0},{16,8},{24,16},{32,24},{40,32},{48,40},{56,48},{64,56},{72,6... | collective-permute-start | bytes 884744 | tf_op jit(solution)/shard_map/ppermute | solution.py:17
  505.8 7.5 %collective-permute-start.11 = (f32[3,24,3,1,128]{4,1,3,2,0:T(8,128)S(1)}, f32[3,24,3,1,128]{4,1,3,2,0:T(8,128)S(1)}, u32[]{:S(2)}, u32[]{:S(2)}) collective-permute-start(f32[3,24,3,1,128]{4,1,3,2,0:T(8,128)S(1)} %pad_maximum_fusion.8), channel_id=1, source_target_pairs={{1,0},{2,1},{3,2},{4,3},{5,4},{6,5},{7,6},{9,8},{10,9},{11,10},{12... | collective-permute-start | bytes 331784 | tf_op jit(solution)/shard_map/ppermute | solution.py:17
  519.2 5.1 copy-start.12
  524.4 6.2 %collective-permute-start.13 = (f32[2,2,8,128]{3,2,1,0:T(8,128)S(1)}, f32[2,2,8,128]{3,2,1,0:T(8,128)S(1)}, u32[]{:S(2)}, u32[]{:S(2)}) collective-permute-start(f32[2,2,8,128]{3,2,1,0:T(8,128)S(1)} %stack.455), channel_id=1, source_target_pairs={{8,0},{16,8},{24,16},{32,24},{40,32},{48,40},{56,48},{64,56},{72,6... | collective-permute-start | bytes 49160 | tf_op jit(solution)/shard_map/ppermute | solution.py:28
  528.7 7.5 %collective-permute-start.12 = (f32[2,2,8,128]{3,2,1,0:T(8,128)S(1)}, f32[2,2,8,128]{3,2,1,0:T(8,128)S(1)}, u32[]{:S(2)}, u32[]{:S(2)}) collective-permute-start(f32[2,2,8,128]{3,2,1,0:T(8,128)S(1)} %stack.455), channel_id=1, source_target_pairs={{0,8},{8,16},{16,24},{24,32},{32,40},{40,48},{48,56},{56,64},{64,7... | collective-permute-start | bytes 49160 | tf_op jit(solution)/shard_map/ppermute | solution.py:27
  536.1 5.3 collective-permute-start.14
  540.1 5.6 %collective-permute-start.15 = (f32[2,6,2,128]{3,2,1,0:T(2,128)S(1)}, f32[2,6,2,128]{3,2,1,0:T(2,128)S(1)}, u32[]{:S(2)}, u32[]{:S(2)}) collective-permute-start(f32[2,6,2,128]{3,2,1,0:T(2,128)S(1)} %get-tuple-element.113), channel_id=1, source_target_pairs={{1,0},{2,1},{3,2},{4,3},{5,4},{6,5},{7,6},{9,8},{10,9},{11,10},{12... | collective-permute-start | bytes 36872 | tf_op jit(solution)/shard_map/ppermute | solution.py:28
where the time goes:
time: 558 us; the launch traced here: 547 us
  blocking collectives  195 us (35%)
  local copies, waits for them, and re-layouts  142 us (25%)
  matrix products  67.7 us (12%)
  waiting for transfers between devices  54.4 us (10%)
  starting transfers between devices  47.9 us (9%)
  other arithmetic  39.2 us (7%)
    psum x2, blocking collectives, local(): lax.psum((block_gram(direction, image_field), block_gram(direction, resid...  132 us
    psum x1, blocking collectives, local(): coupling = lax.psum(block_gram(image_field, scaled_res), ('gx', 'gy'))  62.4 us
    reshape x8, local copies, waits for them, and re-layouts, corner_stack(): return stacked.reshape((24,) + stacked.shape[2:])  59.9 us
    another operation x16, local copies, waits for them, and re-layouts, corner_stack(): stacked = jnp.stack(pieces, 0)  52.4 us
    dot_general x8, matrix products, element_forces(): jnp.einsum('ab,bcxyz->acxyz', element_stiff, gathered, precision=lax.Prec...  46.9 us
    unnamed x55, local copies, waits for them, and re-layouts  29.4 us
    ppermute x6, waiting for transfers between devices, extended_2(): after = lax.ppermute(leading, axis, down)  21.1 us
    ppermute x6, starting transfers between devices, extended_2(): after = lax.ppermute(leading, axis, down)  20.2 us
  transfers between devices with their start and end apart: 16, of which 15 were waited for; matrix products, arithmetic and copies ran while one was open for 1% of the time, Pallas kernels for 0%

commit v1 on v0

--- a/solution.py
+++ b/solution.py
@@ -213,7 +213,9 @@
         residual = residual - combine(image_field, step_alpha)
         if iteration + 1 < ITERS:
             scaled_res = inverse * residual
-            coupling = lax.psum(block_gram(image_field, scaled_res), ("gx", "gy"))
+            part = block_gram(image_field, scaled_res)
+            shards = lax.all_gather(part, ("gx", "gy"), axis=0, tiled=False)
+            coupling = shards.sum(axis=0)
             step_beta = -jax.scipy.linalg.cho_solve((factor, True), coupling)
             direction = scaled_res + combine(direction, step_beta)
     masked_sol = free_mask * solution

time: 558 us -> 806 us (1.44)
  blocking collectives: 195 us -> 443 us
    all_gather x0 -> x1, blocking collectives: none -> 282 us  [local(): shards = lax.all_gather(part, ('gx', 'gy'), axis=0, tiled=False)]
    psum x1 -> x0, blocking collectives: 62.4 us -> none  [local(): coupling = lax.psum(block_gram(image_field, scaled_res), ('gx', 'gy'))]
    psum x2, blocking collectives: 132 us -> 161 us  [local(): lax.psum((block_gram(direction, image_field), block_gram(direction, resid...]
    unnamed x55 -> x57, local copies, waits for them, and re-layouts: 29.4 us -> 29.4 us
  transfers between devices with their start and end apart: 16 -> 16, of which waited for: 15 -> 15; matrix products, arithmetic and copies ran while one was open for 1% -> 0% of each run, Pallas kernels for 0% -> 0%
where the time goes in v1:
time: 806 us; the launch traced here: 795 us
  blocking collectives  443 us (55%)
  local copies, waits for them, and re-layouts  142 us (18%)
  matrix products  67.7 us (8%)
  waiting for transfers between devices  50.6 us (6%)
  starting transfers between devices  50 us (6%)
  other arithmetic  40.3 us (5%)
    all_gather x1, blocking collectives, local(): shards = lax.all_gather(part, ('gx', 'gy'), axis=0, tiled=False)  282 us
    psum x2, blocking collectives, local(): lax.psum((block_gram(direction, image_field), block_gram(direction, resid...  161 us
    reshape x8, local copies, waits for them, and re-layouts, corner_stack(): return stacked.reshape((24,) + stacked.shape[2:])  59.8 us
    another operation x16, local copies, waits for them, and re-layouts, corner_stack(): stacked = jnp.stack(pieces, 0)  52.3 us
    dot_general x8, matrix products, element_forces(): jnp.einsum('ab,bcxyz->acxyz', element_stiff, gathered, precision=lax.Prec...  46.9 us
    unnamed x57, local copies, waits for them, and re-layouts  29.4 us
    ppermute x6, starting transfers between devices, extended_2(): after = lax.ppermute(leading, axis, down)  22 us
    ppermute x6, waiting for transfers between devices, extended_2(): after = lax.ppermute(leading, axis, down)  19.4 us
  transfers between devices with their start and end apart: 16, of which 15 were waited for; matrix products, arithmetic and copies ran while one was open for 0% of the time, Pallas kernels for 0%

profile of v1, /device:TPU:8, one launch (start us, length us, event | category | flops | bytes accessed | tf_op | source)
XLA Modules:
  0.0 795.0 jit_solution(10863054144200587620)
XLA Ops:
  2.6 5.4 collective-permute-done
  17.1 6.0 collective-permute-start.3
  36.6 7.4 collective-permute-done.5
  67.8 7.6 reshape.547
  77.8 6.4 copy.37
  84.2 7.4 reshape.550
  91.6 7.8 multiply_bitcast_fusion.7
  99.4 5.0 multiply_bitcast_fusion.4
  108.4 7.7 reshape.549
  116.1 7.6 multiply_bitcast_fusion.5
  123.7 6.5 copy.35
  130.2 7.4 reshape.548
  137.6 5.3 multiply_bitcast_fusion.6
  142.9 5.5 slice_add_fusion.28
  155.7 67.5 %all-reduce.7 = (f32[24,24]{1,0:T(8,128)S(1)}, f32[24,24]{0,1:T(8,128)S(1)}) all-reduce(f32[24,24]{1,0:T(8,128)S(1)} %convolution_bitcast_fusion.5, f32[24,24]{0,1:T(8,128)S(1)} %convolution_bitcast_fusion.6), channel_id=1, replica_groups=mesh['gx'=16,'gy'=8] {'gx','gy'}, use_global_device_ids=true, to_apply=%region_3.5 | all-reduce | flops 1152 | bytes 9216 | tf_op jit(solution)/shard_map/psum | solution.py:206
  233.1 281.8 %all-gather = f32[3072,24]{1,0:T(8,128)S(1)} all-gather(f32[24,24]{1,0:T(8,128)S(1)} %convolution_bitcast_fusion.3), channel_id=2, replica_groups=mesh['gx'=16,'gy'=8] {'gx','gy'}, dimensions={0}, use_global_device_ids=true | all-gather | bytes 297216 | tf_op jit(solution)/shard_map/all_gather | solution.py:217
  520.2 6.0 collective-permute-start.7
  568.5 7.4 reshape.551
  575.9 5.4 multiply_bitcast_fusion.3
  584.2 6.4 copy.54
  590.6 7.4 reshape.554
  598.0 5.3 multiply_bitcast_fusion
  603.8 6.4 copy.53
  610.2 7.4 reshape.553
  617.5 5.3 multiply_bitcast_fusion.1
  623.3 6.5 copy.52
  629.8 7.6 reshape.552
  637.4 5.3 multiply_bitcast_fusion.2
  644.8 93.8 %all-reduce.6 = (f32[24,24]{1,0:T(8,128)S(1)}, f32[24,24]{0,1:T(8,128)S(1)}) all-reduce(f32[24,24]{1,0:T(8,128)S(1)} %convolution_bitcast_fusion.1, f32[24,24]{0,1:T(8,128)S(1)} %convolution_bitcast_fusion.2), channel_id=1, replica_groups=mesh['gx'=16,'gy'=8] {'gx','gy'}, use_global_device_ids=true, to_apply=%region_6.9 | all-reduce | flops 1152 | bytes 9216 | tf_op jit(solution)/shard_map/psum | solution.py:206
  754.2 5.5 collective-permute-done.11
  770.8 5.7 collective-permute-start.13
  778.4 5.5 collective-permute-done.12
  (163 shorter events, 164.7 us)
Async XLA Ops:
  0.7 7.3 collective-permute-start
  8.0 4.7 collective-permute-start.1
  15.1 12.7 %collective-permute-start.2 = (f32[3,24,1,8,128]{4,0,3,2,1:T(4,128)S(1)}, f32[3,24,1,8,128]{4,0,3,2,1:T(4,128)S(1)}, u32[]{:S(2)}, u32[]{:S(2)}) collective-permute-start(f32[3,24,1,8,128]{4,0,3,2,1:T(4,128)S(1)} %get-tuple-element.101), channel_id=1, source_target_pairs={{0,8},{8,16},{16,24},{24,32},{32,40},{40,48},{48,56},{56,64},{64,7... | collective-permute-start | bytes 884744 | tf_op jit(solution)/shard_map/ppermute | solution.py:27
  17.1 11.3 %collective-permute-start.3 = (f32[3,24,1,8,128]{4,0,3,2,1:T(4,128)S(1)}, f32[3,24,1,8,128]{4,0,3,2,1:T(4,128)S(1)}, u32[]{:S(2)}, u32[]{:S(2)}) collective-permute-start(f32[3,24,1,8,128]{4,0,3,2,1:T(4,128)S(1)} %get-tuple-element.102), channel_id=1, source_target_pairs={{8,0},{16,8},{24,16},{32,24},{40,32},{48,40},{56,48},{64,56},{72,6... | collective-permute-start | bytes 884744 | tf_op jit(solution)/shard_map/ppermute | solution.py:28
  28.5 8.1 %collective-permute-start.4 = (f32[3,24,4,1,128]{4,0,3,2,1:T(4,128)S(1)}, f32[3,24,4,1,128]{4,0,3,2,1:T(4,128)S(1)}, u32[]{:S(2)}, u32[]{:S(2)}) collective-permute-start(f32[3,24,4,1,128]{4,0,3,2,1:T(4,128)S(1)} %get-tuple-element.79), channel_id=1, source_target_pairs={{0,1},{1,2},{2,3},{3,4},{4,5},{5,6},{6,7},{8,9},{9,10},{10,11},{11... | collective-permute-start | bytes 442376 | tf_op jit(solution)/shard_map/ppermute | solution.py:27
  32.7 11.3 %collective-permute-start.5 = (f32[3,24,4,1,128]{4,0,3,2,1:T(4,128)S(1)}, f32[3,24,4,1,128]{4,0,3,2,1:T(4,128)S(1)}, u32[]{:S(2)}, u32[]{:S(2)}) collective-permute-start(f32[3,24,4,1,128]{4,0,3,2,1:T(4,128)S(1)} %get-tuple-element.80), channel_id=1, source_target_pairs={{1,0},{2,1},{3,2},{4,3},{5,4},{6,5},{7,6},{9,8},{10,9},{11,10},{12... | collective-permute-start | bytes 442376 | tf_op jit(solution)/shard_map/ppermute | solution.py:28
  48.2 7.3 copy-start.1
  56.9 2.3 copy-start.3
  59.2 2.4 copy-start.5
  61.6 2.3 copy-start.6
  84.2 7.4 copy-start.12
  91.6 7.8 copy-start.2
  91.6 12.8 %slice-start = ((s8[5308416]{0:T(1024)(128)(4,1)}), s8[4194304]{0:T(1024)(128)(4,1)S(1)}, s32[]{:S(2)}) async-start(s8[5308416]{0:T(1024)(128)(4,1)} %bitcast.1303), calls=%async_computation | async-start | bytes 8388608
  99.4 5.0 slice-start.1
  142.9 9.4 %copy-start.10 = (f32[3,24,2,8,128]{4,3,2,1,0:T(8,128)S(1)}, f32[3,24,2,8,128]{4,3,2,1,0:T(8,128)}, u32[]{:S(2)}) copy-start(f32[3,24,2,8,128]{4,3,2,1,0:T(8,128)} %param.7) | copy-start | bytes 1769476
  231.7 1.3 copy-start.9
  516.3 22.4 %copy-start.11 = (f32[3,24,2,8,128]{4,0,3,2,1:T(4,128)S(1)}, f32[3,24,2,8,128]{4,0,3,2,1:T(4,128)}, u32[]{:S(2)}) copy-start(f32[3,24,2,8,128]{4,0,3,2,1:T(4,128)} %get-tuple-element.14) | copy-start | bytes 1769476
  518.3 11.5 %collective-permute-start.6 = (f32[3,24,1,8,128]{4,0,3,2,1:T(4,128)S(1)}, f32[3,24,1,8,128]{4,0,3,2,1:T(4,128)S(1)}, u32[]{:S(2)}, u32[]{:S(2)}) collective-permute-start(f32[3,24,1,8,128]{4,0,3,2,1:T(4,128)S(1)} %get-tuple-element.99), channel_id=1, source_target_pairs={{0,8},{8,16},{16,24},{24,32},{32,40},{40,48},{48,56},{56,64},{64,7... | collective-permute-start | bytes 884744 | tf_op jit(solution)/shard_map/ppermute | solution.py:27
  520.2 12.4 %collective-permute-start.7 = (f32[3,24,1,8,128]{4,0,3,2,1:T(4,128)S(1)}, f32[3,24,1,8,128]{4,0,3,2,1:T(4,128)S(1)}, u32[]{:S(2)}, u32[]{:S(2)}) collective-permute-start(f32[3,24,1,8,128]{4,0,3,2,1:T(4,128)S(1)} %get-tuple-element.100), channel_id=1, source_target_pairs={{8,0},{16,8},{24,16},{32,24},{40,32},{48,40},{56,48},{64,56},{72,6... | collective-permute-start | bytes 884744 | tf_op jit(solution)/shard_map/ppermute | solution.py:28
  532.8 7.5 collective-permute-start.8
  537.1 7.6 collective-permute-start.9
  548.8 7.3 copy-start
  557.6 2.3 copy-start.4
  559.9 2.4 copy-start.7
  562.2 2.3 copy-start.8
  745.4 7.1 collective-permute-start.10
  752.6 7.1 collective-permute-start.11
  765.6 5.1 copy-start.13
  770.8 7.6 collective-permute-start.13
  776.4 7.5 collective-permute-start.12
  783.9 5.3 collective-permute-start.14
  787.9 5.6 collective-permute-start.15
